TPU v7x, 32 devices: a whole 2x2x4 slice. The times are simulated.
32 devices in a mesh: row: 8 (over z, y), col: 4 (over x, core).
Axes of the slice: x: 2, y: 2, z: 4, core: 2. Of those that a mesh axis runs over, the one named last changes fastest.
Arguments:
- trail_adjoint: float32 [4096, 4096], P('row', 'col'), may hold values from -6 to 6
- lower_new: float32 [4096, 256], P('row', 'col'), may hold values from -0.09375 to 0.09375
- upper_new: float32 [256, 4096], P('row', 'col'), may hold values from -0.09375 to 0.09375
- lower_old_top: float32 [256, 256], replicated, may hold values from -0.375 to 0.375
- lower_old: float32 [4096, 256], P('row', 'col'), may hold values from -0.09375 to 0.09375
- upper_old_left: float32 [256, 256], replicated, may hold values from -0.375 to 0.375
- upper_old: float32 [256, 4096], P('row', 'col'), may hold values from -0.09375 to 0.09375
- diag_lower_new: float32 [256, 256], replicated, as said below
- diag_upper_new: float32 [256, 256], replicated, as said below
- inverse_lower_new: float32 [256, 256], replicated, as said below
- inverse_upper_new: float32 [256, 256], replicated, as said below
- diag_lower_old: float32 [256, 256], replicated, as said below
- diag_upper_old: float32 [256, 256], replicated, as said below
- inverse_lower_old: float32 [256, 256], replicated, as said below
- inverse_upper_old: float32 [256, 256], replicated, as said below
Outputs:
- corner_old: float32 [256, 256], replicated
- strip_top: float32 [256, 256], replicated
- strip_bottom: float32 [4096, 256], P(('row', 'col'))
- band_left: float32 [256, 256], replicated
- band_right: float32 [256, 4096], P(None, 'col')
Inputs may be any that keep to these rules, and one draw needn't show every extreme that they name: `diag_lower_new`: unit lower triangular. `diag_upper_new`: upper triangular, diagonal from 1 to 2. `inverse_lower_new`: the inverse of diag_lower_new. `inverse_upper_new`: the inverse of diag_upper_new. `diag_lower_old`: unit lower triangular. `diag_upper_old`: upper triangular, diagonal from 1 to 2. `inverse_lower_old`: the inverse of diag_lower_old. `inverse_upper_old`: the inverse of diag_upper_old.
All inputs are finite; a program needn't handle non-finite values.
Results may differ from a plain program's by a relative error of at most 0.000075.
Values sent between devices are 32-bit elements; how exact they have to be, the bound alone decides.
A program may use at most 128 MiB of HBM per device.

v0:
```python
import jax
import jax.numpy as jnp
from jax import lax
from jax.sharding import PartitionSpec as P

precise = lax.Precision.HIGHEST


def times_trans(left, right):
    return lax.dot_general(left, right, (((1,), (1,)), ((), ())), precision=precise)


def trans_times(left, right):
    return lax.dot_general(left, right, (((0,), (0,)), ((), ())), precision=precise)


def diag_adjoint(lower_factor, upper_factor, lower_inverse, upper_inverse, lower_grad, upper_grad):
    inner = jnp.tril(trans_times(lower_factor, lower_grad), -1) + jnp.triu(
        times_trans(upper_grad, upper_factor)
    )
    return times_trans(trans_times(lower_inverse, inner), upper_inverse)


def upper_inner(terms):
    summed = lax.psum(terms, "col")
    return summed


def lower_inner(terms):
    summed = lax.psum(terms, "row")
    return summed


def body(
    trail_adjoint,
    lower_new,
    upper_new,
    lower_old_top,
    lower_old,
    upper_old_left,
    upper_old,
    diag_lower_new,
    diag_upper_new,
    inverse_lower_new,
    inverse_upper_new,
    diag_lower_old,
    diag_upper_old,
    inverse_lower_old,
    inverse_upper_old,
):
    width = inverse_lower_new.shape[0]
    lower_full_new, lower_full_old = (
        lax.all_gather(lower_new, "col", axis=1, tiled=True),
        lax.all_gather(lower_old, "col", axis=1, tiled=True),
    )
    upper_full_new, upper_full_old = (
        lax.all_gather(upper_new, "row", axis=0, tiled=True),
        lax.all_gather(upper_old, "row", axis=0, tiled=True),
    )
    lower_stack = jnp.concatenate((lower_full_new, lower_full_old), axis=1)
    upper_stack = jnp.concatenate((upper_full_new, upper_full_old), axis=0)
    portion = trail_adjoint.shape[0] // lax.axis_size("col")
    offset = lax.axis_index("col") * portion
    lower_adj = lax.psum(-times_trans(trail_adjoint, upper_stack), "col")
    lower_adj_new = lower_adj[:, :width]
    lower_adj_old = lower_adj[:, width:]
    strip_new = times_trans(lower_adj_new, inverse_upper_new)
    upper_adj = lax.psum(-trans_times(lower_stack, trail_adjoint), "row")
    band_new = trans_times(inverse_lower_new, upper_adj[:width])
    outer_new = upper_inner(
        (times_trans(band_new, upper_full_new), times_trans(band_new, upper_full_old))
    )
    inner_new = lower_inner(
        (trans_times(lower_full_new, strip_new), trans_times(lower_full_old, strip_new))
    )
    corner_new = diag_adjoint(
        diag_lower_new,
        diag_upper_new,
        inverse_lower_new,
        inverse_upper_new,
        -outer_new[0],
        -inner_new[0],
    )
    strip_top = times_trans(
        -(times_trans(corner_new, upper_old_left) + outer_new[1]), inverse_upper_old
    )
    strip_bottom = times_trans(
        lower_adj_old - times_trans(strip_new, upper_old_left), inverse_upper_old
    )
    band_left = trans_times(
        inverse_lower_old, -(trans_times(lower_old_top, corner_new) + inner_new[1])
    )
    band_right = trans_times(
        inverse_lower_old, upper_adj[width:] - trans_times(lower_old_top, band_new)
    )
    outer_old = upper_inner(times_trans(band_right, upper_full_old))
    inner_old = lower_inner(trans_times(lower_full_old, strip_bottom))
    lower_grad = -(times_trans(band_left, upper_old_left) + outer_old)
    upper_grad = -(trans_times(lower_old_top, strip_top) + inner_old)
    corner_old = diag_adjoint(
        diag_lower_old, diag_upper_old, inverse_lower_old, inverse_upper_old, lower_grad, upper_grad
    )
    strip_bottom = lax.dynamic_slice_in_dim(strip_bottom, offset, portion, 0)
    return (corner_old, strip_top, strip_bottom, band_left, band_right)


def solution(mesh):
    return jax.shard_map(
        body,
        mesh=mesh,
        in_specs=(
            P("row", "col"),
            P("row", "col"),
            P("row", "col"),
            P(),
            P("row", "col"),
            P(),
            P("row", "col"),
            P(),
            P(),
            P(),
            P(),
            P(),
            P(),
            P(),
            P(),
        ),
        out_specs=(P(), P(), P(("row", "col"), None), P(), P(None, "col")),
        check_vma=False,
    )
```

profile of v0, /device:TPU:0, one launch (start us, length us, event | category | flops | bytes accessed | tf_op | source)
XLA Modules:
  0.0 336.3 jit_solution(6877117094611444565)
XLA Ops:
  8.7 8.9 %all_gather.13 = f32[512,256]{0,1:T(8,128)S(1)} all-gather(f32[512,64]{0,1:T(8,128)} %param.19), channel_id=1, replica_groups=mesh['row'=8,'col'=4] {'col'}, dimensions={1}, use_global_device_ids=true | all-gather | bytes 655360 | tf_op jit(solution)/shard_map/all_gather | solution.py:54
  17.6 35.6 %all-gather.3.cloned.1.call-done = f32[256,1024]{1,0:T(8,128)} async-done(((f32[32,1024]{1,0:T(8,128)}), f32[256,1024]{1,0:T(8,128)}) %all-gather.3.cloned.1.call-update) | async-done | bytes 1048592 | tf_op jit(solution)/shard_map/all_gather | solution.py:57
  53.1 41.1 %all-gather.5.cloned.1.call-done = f32[256,1024]{1,0:T(8,128)} async-done(((f32[32,1024]{1,0:T(8,128)}), f32[256,1024]{1,0:T(8,128)}) %all-gather.5.cloned.1.call-update) | async-done | bytes 1048592 | tf_op jit(solution)/shard_map/all_gather | solution.py:58
  94.3 6.0 %fusion.7 = f32[512,512]{0,1:T(8,128)} fusion(f32[512,1024]{1,0:T(8,128)S(1)} %copy-done, f32[256,1024]{1,0:T(8,128)} %all-gather.5.cloned.1.call-done, f32[256,1024]{1,0:T(8,128)} %all-gather.3.cloned.1.call-done), kind=kOutput, calls=%fused_computation.6 | convolution fusion | flops 3222011904 | bytes 5242880 | tf_op jit(solution)/shard_map/dot_general | solution.py:10
  100.4 7.8 %all_gather.12 = f32[512,256]{0,1:T(8,128)S(1)} all-gather(f32[512,64]{0,1:T(8,128)S(1)} %copy-done.22), channel_id=1, replica_groups=mesh['row'=8,'col'=4] {'col'}, dimensions={1}, use_global_device_ids=true | all-gather | bytes 655360 | tf_op jit(solution)/shard_map/all_gather | solution.py:53
  108.2 4.9 %convolution_negate_fusion = f32[512,1024]{1,0:T(8,128)} fusion(f32[512,1024]{1,0:T(8,128)S(1)} %copy-done, f32[512,256]{0,1:T(8,128)S(1)} %all_gather.13, f32[512,256]{0,1:T(8,128)S(1)} %all_gather.12), kind=kOutput, calls=%fused_computation.4 | convolution fusion | flops 3222011904 | bytes 5242880 | tf_op jit(solution)/shard_map/dot_general | solution.py:14
  113.2 22.4 %all-reduce.6.cloned.1.call-done = f32[512,512]{0,1:T(8,128)} async-done(((f32[512,512]{0,1:T(8,128)}), f32[512,512]{0,1:T(8,128)}) %all-reduce.6.cloned.1.call-update) | async-done | bytes 1048592 | tf_op jit(solution)/shard_map/psum | solution.py:64
  135.5 2.2 fusion.26
  137.7 1.7 convolution_bitcast_fusion.4
  139.5 1.7 convolution_bitcast_fusion.6
  143.7 1.7 convolution_bitcast_fusion.1
  145.7 123.1 %all-reduce.8.cloned.1.call-done = (f32[512,1024]{1,0:T(8,128)}, f32[256,256]{0,1:T(8,128)}, f32[256,256]{0,1:T(8,128)}, f32[256,256]{0,1:T(8,128)}) async-done(((f32[512,1024]{1,0:T(8,128)}, f32[256,256]{0,1:T(8,128)}, f32[256,256]{0,1:T(8,128)}, f32[256,256]{0,1:T(8,128)}), (f32[512,1024]{1,0:T(8,128)}, f32[256,256]{0,1:T(8,128)}, f32[256,256]{0,1:T(8,128)}, ...) | async-done | bytes 2883600 | tf_op jit(solution)/shard_map/psum | solution.py:68
  268.8 3.2 fusion.21
  273.2 1.8 fusion.36
  275.0 2.5 fusion.32
  277.5 2.5 fusion.38
  280.0 2.5 fusion.37
  282.6 1.6 constant_dynamic-slice_fusion
  284.2 1.3 copy.21
  285.5 31.3 %all-reduce.10.cloned.1.call-done = (f32[256,256]{1,0:T(8,128)}, f32[256,256]{1,0:T(8,128)}, f32[256,256]{1,0:T(8,128)}) async-done(((f32[256,256]{1,0:T(8,128)}, f32[256,256]{1,0:T(8,128)}, f32[256,256]{1,0:T(8,128)}), (f32[256,256]{1,0:T(8,128)}, f32[256,256]{1,0:T(8,128)}, f32[256,256]{1,0:T(8,128)})) %all-reduce.10.cloned.1.call-update) | async-done | bytes 786448 | tf_op jit(solution)/shard_map/psum | solution.py:25
  316.8 1.7 fusion.20
  318.5 1.6 fusion.19
  320.2 1.8 fusion.33
  327.6 1.3 fusion.42
  (71 shorter events, 11.7 us)
Async XLA Ops:
  7.2 87.1 %copy-start = (f32[512,1024]{1,0:T(8,128)S(1)}, f32[512,1024]{1,0:T(8,128)}, u32[]{:S(2)}) copy-start(f32[512,1024]{1,0:T(8,128)} %param.15) | copy-start | bytes 6291460
  7.2 46.0 %all-gather.3.cloned.1.call-start = ((), (), s32[]{:S(2)}) async-start(), calls=%async_computation | async-start | bytes 1179648 | tf_op jit(solution)/shard_map/all_gather | solution.py:57
  7.9 86.4 %all-gather.5.cloned.1.call-start = ((), (), s32[]{:S(2)}) async-start(), calls=%async_computation.1 | async-start | bytes 1179648 | tf_op jit(solution)/shard_map/all_gather | solution.py:58
  8.7 126.9 %all-reduce.6.cloned.1.call-start = ((), (), s32[]{:S(2)}) async-start(), calls=%async_computation.2 | async-start | bytes 2097152 | tf_op jit(solution)/shard_map/psum | solution.py:64
  17.6 82.8 %copy-start.22 = (f32[512,64]{0,1:T(8,128)S(1)}, f32[512,64]{0,1:T(8,128)}, u32[]{:S(2)}) copy-start(f32[512,64]{0,1:T(8,128)} %param.16) | copy-start | bytes 393220
  100.4 168.4 %all-reduce.8.cloned.1.call-start = ((), (), s32[]{:S(2)}) async-start(), calls=%async_computation.3 | async-start | bytes 5767168 | tf_op jit(solution)/shard_map/psum | solution.py:68
  113.2 28.0 %copy-start.7 = (f32[256,256]{1,0:T(8,128)S(1)}, f32[256,256]{1,0:T(8,128)}, u32[]{:S(2)}) copy-start(f32[256,256]{1,0:T(8,128)} %param.20) | copy-start | bytes 786436
  135.5 5.7 %copy-start.14 = (f32[512,512]{0,1:T(8,128)S(1)}, f32[512,512]{0,1:T(8,128)}, u32[]{:S(2)}) copy-start(f32[512,512]{0,1:T(8,128)} %all-reduce.6.cloned.1.call-done) | copy-start | bytes 3145732
  137.7 4.2 %copy-start.5 = (f32[256,256]{1,0:T(8,128)S(1)}, f32[256,256]{1,0:T(8,128)}, u32[]{:S(2)}) copy-start(f32[256,256]{1,0:T(8,128)} %param.29) | copy-start | bytes 786436
  143.7 125.1 %copy-start.12 = (f32[256,256]{1,0:T(8,128)S(1)}, f32[256,256]{1,0:T(8,128)}, u32[]{:S(2)}) copy-start(f32[256,256]{1,0:T(8,128)} %param.24) | copy-start | bytes 786436
  145.4 126.6 %copy-start.9 = (f32[256,256]{1,0:T(8,128)S(1)}, f32[256,256]{1,0:T(8,128)}, u32[]{:S(2)}) copy-start(f32[256,256]{1,0:T(8,128)} %param.18) | copy-start | bytes 786436
  145.4 171.4 %all-reduce.10.cloned.1.call-start = ((), (), s32[]{:S(2)}) async-start(), calls=%async_computation.4 | async-start | bytes 1572864 | tf_op jit(solution)/shard_map/psum | solution.py:25
  268.8 3.2 copy-start.11
  272.0 3.0 copy-start.2
  273.2 4.4 %copy-start.1 = (f32[256,1024]{1,0:T(8,128)S(1)}, f32[256,1024]{1,0:T(8,128)}, u32[]{:S(2)}) copy-start(f32[256,1024]{1,0:T(8,128)} %all-gather.5.cloned.1.call-done) | copy-start | bytes 3145732
  285.5 36.5 %copy-start.13 = (f32[256,256]{1,0:T(8,128)S(1)}, f32[256,256]{1,0:T(8,128)}, u32[]{:S(2)}) copy-start(f32[256,256]{1,0:T(8,128)} %param.25) | copy-start | bytes 786436
  285.5 37.1 %copy-start.8 = (f32[256,256]{1,0:T(8,128)S(1)}, f32[256,256]{1,0:T(8,128)}, u32[]{:S(2)}) copy-start(f32[256,256]{1,0:T(8,128)} %param.20) | copy-start | bytes 786436
  316.8 5.8 %copy-start.21 = (f32[256,256]{1,0:T(8,128)S(1)}, f32[256,256]{1,0:T(8,128)}, u32[]{:S(2)}) copy-start(f32[256,256]{1,0:T(8,128)} %get-tuple-element.16) | copy-start | bytes 786436
  316.8 6.3 %copy-start.10 = (f32[256,256]{1,0:T(8,128)S(1)}, f32[256,256]{1,0:T(8,128)}, u32[]{:S(2)}) copy-start(f32[256,256]{1,0:T(8,128)} %param.18) | copy-start | bytes 786436
  316.8 6.3 %copy-start.19 = (f32[256,256]{0,1:T(8,128)S(1)}, f32[256,256]{0,1:T(8,128)}, u32[]{:S(2)}) copy-start(f32[256,256]{0,1:T(8,128)} %get-tuple-element.11) | copy-start | bytes 786436
  320.1 4.0 %copy-start.6 = (f32[256,256]{1,0:T(8,128)S(1)}, f32[256,256]{1,0:T(8,128)}, u32[]{:S(2)}) copy-start(f32[256,256]{1,0:T(8,128)} %param.29) | copy-start | bytes 786436
  322.0 2.5 copy-start.18
  323.7 2.7 copy-start.16
  324.6 3.1 copy-start.15
  (4 other events, 6.1 us)
Sparse Core Ops, SparseCore 0:
  10.1 42.9 all-gather.2
  55.3 38.9 all-gather.4
  100.5 34.9 all-reduce.5
  145.6 123.1 all-reduce.7
  282.7 34.0 all-reduce.9
where the time goes:
time: 337 us; the launch traced here: 336 us
  waiting for transfers between devices  255 us (76%)
  matrix products  45.5 us (14%)
  blocking collectives  16.7 us (5%)
  between operations  14.2 us (4%)
  local copies, waits for them, and re-layouts  4.61 us (1%)
    psum x1, waiting for transfers between devices, body(): upper_adj = lax.psum(-trans_times(lower_stack, trail_adjoint), 'row')  123 us
    all_gather x1, waiting for transfers between devices, body(): lax.all_gather(upper_old, 'row', axis=0, tiled=True)  41.1 us
    all_gather x1, waiting for transfers between devices, body(): lax.all_gather(upper_new, 'row', axis=0, tiled=True)  35.6 us
    psum x1, waiting for transfers between devices, upper_inner(): summed = lax.psum(terms, 'col')  31.3 us
    dot_general x14, matrix products, times_trans(): lax.dot_general(left, right, (((1,), (1,)), ((), ())), precision=precise)  23 us
    dot_general x14, matrix products, trans_times(): lax.dot_general(left, right, (((0,), (0,)), ((), ())), precision=precise)  22.5 us
    psum x1, waiting for transfers between devices, body(): lower_adj = lax.psum(-times_trans(trail_adjoint, upper_stack), 'col')  22.4 us
    all_gather x1, blocking collectives, body(): lax.all_gather(lower_old, 'col', axis=1, tiled=True)  8.86 us
  transfers between devices with their start and end apart: 5, of which 5 were waited for; matrix products, arithmetic and copies ran while one was open for 2% of the time, Pallas kernels for 0%

commit v1 on v0

--- a/solution.py
+++ b/solution.py
@@ -54,7 +54,9 @@
         lax.all_gather(lower_old, "col", axis=1, tiled=True),
     )
     upper_full_new, upper_full_old = (
-        lax.all_gather(upper_new, "row", axis=0, tiled=True),
+        jnp.concatenate(
+            lax.all_to_all(jnp.stack([upper_new] * lax.axis_size("row")), "row", 0, 0), axis=0
+        ),
         lax.all_gather(upper_old, "row", axis=0, tiled=True),
     )
     lower_stack = jnp.concatenate((lower_full_new, lower_full_old), axis=1)

time: 337 us -> 302 us (0.90)
  waiting for transfers between devices: 255 us -> 210 us
  starting transfers between devices: 0.42 us -> 7.69 us
    all_gather x1 -> x0, waiting for transfers between devices: 35.6 us -> none  [body(): lax.all_gather(upper_new, 'row', axis=0, tiled=True)]
    all_to_all x0 -> x1, starting transfers between devices: none -> 7.31 us  [body(): lax.all_to_all(jnp.stack([upper_new] * lax.axis_size('row')), 'row', 0, 0)]
    all_gather x1, waiting for transfers between devices: 41.1 us -> 34 us  [body(): lax.all_gather(upper_old, 'row', axis=0, tiled=True)]
  transfers between devices with their start and end apart: 5 -> 5, of which waited for: 5 -> 4; matrix products, arithmetic and copies ran while one was open for 2% -> 4% of each run, Pallas kernels for 0% -> 0%
where the time goes in v1:
time: 302 us
  waiting for transfers between devices  210 us (70%)
  matrix products  47.4 us (16%)
  blocking collectives  15.3 us (5%)
  between operations  14.2 us (5%)
  starting transfers between devices  7.69 us (3%)
  local copies, waits for them, and re-layouts  7.41 us (2%)
    psum x1, waiting for transfers between devices, body(): upper_adj = lax.psum(-trans_times(lower_stack, trail_adjoint), 'row')  123 us
    all_gather x1, waiting for transfers between devices, body(): lax.all_gather(upper_old, 'row', axis=0, tiled=True)  34 us
    psum x1, waiting for transfers between devices, upper_inner(): summed = lax.psum(terms, 'col')  31.3 us
    dot_general x14, matrix products, trans_times(): lax.dot_general(left, right, (((0,), (0,)), ((), ())), precision=precise)  24.6 us
    dot_general x14, matrix products, times_trans(): lax.dot_general(left, right, (((1,), (1,)), ((), ())), precision=precise)  22.7 us
    psum x1, waiting for transfers between devices, body(): lower_adj = lax.psum(-times_trans(trail_adjoint, upper_stack), 'col')  20.7 us
    all_gather x1, blocking collectives, body(): lax.all_gather(lower_new, 'col', axis=1, tiled=True)  7.72 us
    all_gather x1, blocking collectives, body(): lax.all_gather(lower_old, 'col', axis=1, tiled=True)  7.62 us
  transfers between devices with their start and end apart: 5, of which 4 were waited for; matrix products, arithmetic and copies ran while one was open for 4% of the time, Pallas kernels for 0%

profile of v1, /device:TPU:0, one launch (start us, length us, event | category | flops | bytes accessed | tf_op | source)
XLA Modules:
  0.0 301.6 jit_solution(4202098936386270104)
XLA Ops:
  7.9 2.0 stack.2
  9.9 7.3 %all-to-all-start = ((f32[8,32,1024]{2,1,0:T(8,128)}), f32[8,32,1024]{2,1,0:T(8,128)S(1)}, u32[]{:S(2)}, u32[]{:S(2)}) async-start(f32[8,32,1024]{2,1,0:T(8,128)} %stack.2), calls=%async_computation | async-start | bytes 2097152 | tf_op jit(solution)/shard_map/all_to_all | solution.py:58
  17.3 7.6 %all_gather.10 = f32[512,256]{0,1:T(8,128)} all-gather(f32[512,64]{0,1:T(8,128)S(1)} %copy-done.24), channel_id=1, replica_groups=mesh['row'=8,'col'=4] {'col'}, dimensions={1}, use_global_device_ids=true | all-gather | bytes 655360 | tf_op jit(solution)/shard_map/all_gather | solution.py:54
  24.9 34.0 %all-gather.2.cloned.1.call-done = f32[256,1024]{1,0:T(8,128)} async-done(((f32[32,1024]{1,0:T(8,128)}), f32[256,1024]{1,0:T(8,128)}) %all-gather.2.cloned.1.call-update) | async-done | bytes 1048592 | tf_op jit(solution)/shard_map/all_gather | solution.py:60
  58.9 5.8 %fusion.7 = f32[512,512]{0,1:T(8,128)} fusion(f32[512,1024]{1,0:T(8,128)S(1)} %copy-done, f32[256,1024]{1,0:T(8,128)} %all-gather.2.cloned.1.call-done, f32[256,1024]{1,0:T(8,128)S(1)} %bitcast.85), kind=kOutput, calls=%fused_computation.6 | convolution fusion | flops 3222011904 | bytes 5242880 | tf_op jit(solution)/shard_map/dot_general | solution.py:10
  64.7 7.7 %all_gather.9 = f32[512,256]{0,1:T(8,128)S(1)} all-gather(f32[512,64]{0,1:T(8,128)S(1)} %copy-done.25), channel_id=1, replica_groups=mesh['row'=8,'col'=4] {'col'}, dimensions={1}, use_global_device_ids=true | all-gather | bytes 655360 | tf_op jit(solution)/shard_map/all_gather | solution.py:53
  73.3 6.0 %convolution_negate_fusion = f32[512,1024]{1,0:T(8,128)} fusion(f32[512,1024]{1,0:T(8,128)S(1)} %copy-done, f32[512,256]{0,1:T(8,128)} %all_gather.10, f32[512,256]{0,1:T(8,128)S(1)} %all_gather.9), kind=kOutput, calls=%fused_computation.4 | convolution fusion | flops 3222011904 | bytes 5242880 | tf_op jit(solution)/shard_map/dot_general | solution.py:14
  79.2 20.7 %all-reduce.6.cloned.1.call-done = f32[512,512]{0,1:T(8,128)} async-done(((f32[512,512]{0,1:T(8,128)}), f32[512,512]{0,1:T(8,128)}) %all-reduce.6.cloned.1.call-update) | async-done | bytes 1048592 | tf_op jit(solution)/shard_map/psum | solution.py:66
  99.9 2.2 fusion.26
  102.1 2.8 convolution_bitcast_fusion.4
  105.0 1.7 convolution_bitcast_fusion.6
  109.2 1.7 convolution_bitcast_fusion.1
  111.2 122.9 %all-reduce.8.cloned.1.call-done = (f32[512,1024]{1,0:T(8,128)}, f32[256,256]{0,1:T(8,128)}, f32[256,256]{0,1:T(8,128)}, f32[256,256]{0,1:T(8,128)}) async-done(((f32[512,1024]{1,0:T(8,128)}, f32[256,256]{0,1:T(8,128)}, f32[256,256]{0,1:T(8,128)}, f32[256,256]{0,1:T(8,128)}), (f32[512,1024]{1,0:T(8,128)}, f32[256,256]{0,1:T(8,128)}, f32[256,256]{0,1:T(8,128)}, ...) | async-done | bytes 2883600 | tf_op jit(solution)/shard_map/psum | solution.py:70
  234.1 3.2 %fusion.21 = f32[1024,256]{1,0:T(8,128)S(1)} fusion(f32[256,256]{1,0:T(8,128)S(1)} %copy-done.14, f32[512,1024]{1,0:T(8,128)} %get-tuple-element.10), kind=kOutput, calls=%fused_computation.31 | convolution fusion | flops 805306368 | bytes 2359296 | tf_op jit(solution)/shard_map/dot_general | solution.py:14
  237.3 2.5 fusion.32
  241.0 1.8 fusion.36
  242.8 2.5 fusion.38
  245.3 2.5 fusion.37
  247.9 1.6 constant_dynamic-slice_fusion
  249.5 1.3 copy.21
  250.8 31.3 %all-reduce.10.cloned.1.call-done = (f32[256,256]{1,0:T(8,128)}, f32[256,256]{1,0:T(8,128)}, f32[256,256]{1,0:T(8,128)}) async-done(((f32[256,256]{1,0:T(8,128)}, f32[256,256]{1,0:T(8,128)}, f32[256,256]{1,0:T(8,128)}), (f32[256,256]{1,0:T(8,128)}, f32[256,256]{1,0:T(8,128)}, f32[256,256]{1,0:T(8,128)})) %all-reduce.10.cloned.1.call-update) | async-done | bytes 786448 | tf_op jit(solution)/shard_map/psum | solution.py:25
  282.1 1.7 fusion.20
  283.8 1.6 fusion.19
  285.4 1.9 fusion.33
  (77 shorter events, 13.1 us)
Async XLA Ops:
  7.2 51.7 %copy-start = (f32[512,1024]{1,0:T(8,128)S(1)}, f32[512,1024]{1,0:T(8,128)}, u32[]{:S(2)}) copy-start(f32[512,1024]{1,0:T(8,128)} %param.15) | copy-start | bytes 6291460
  7.2 10.1 %copy-start.24 = (f32[512,64]{0,1:T(8,128)S(1)}, f32[512,64]{0,1:T(8,128)}, u32[]{:S(2)}) copy-start(f32[512,64]{0,1:T(8,128)} %param.19) | copy-start | bytes 393220
  7.2 51.7 %all-gather.2.cloned.1.call-start = ((), (), s32[]{:S(2)}) async-start(), calls=%async_computation.1 | async-start | bytes 1179648 | tf_op jit(solution)/shard_map/all_gather | solution.py:60
  9.9 49.0 %all-to-all-start = ((f32[8,32,1024]{2,1,0:T(8,128)}), f32[8,32,1024]{2,1,0:T(8,128)S(1)}, u32[]{:S(2)}, u32[]{:S(2)}) async-start(f32[8,32,1024]{2,1,0:T(8,128)} %stack.2), calls=%async_computation | async-start | bytes 2097152 | tf_op jit(solution)/shard_map/all_to_all | solution.py:58
  17.2 82.7 %all-reduce.6.cloned.1.call-start = ((), (), s32[]{:S(2)}) async-start(), calls=%async_computation.2 | async-start | bytes 2097152 | tf_op jit(solution)/shard_map/psum | solution.py:66
  58.9 5.8 %copy-start.25 = (f32[512,64]{0,1:T(8,128)S(1)}, f32[512,64]{0,1:T(8,128)}, u32[]{:S(2)}) copy-start(f32[512,64]{0,1:T(8,128)} %param.16) | copy-start | bytes 393220
  64.7 169.4 %all-reduce.8.cloned.1.call-start = ((), (), s32[]{:S(2)}) async-start(), calls=%async_computation.3 | async-start | bytes 5767168 | tf_op jit(solution)/shard_map/psum | solution.py:70
  79.2 27.5 %copy-start.9 = (f32[256,256]{1,0:T(8,128)S(1)}, f32[256,256]{1,0:T(8,128)}, u32[]{:S(2)}) copy-start(f32[256,256]{1,0:T(8,128)} %param.20) | copy-start | bytes 786436
  99.9 5.1 %copy-start.4 = (f32[512,256]{0,1:T(8,128)S(1)}, f32[512,256]{0,1:T(8,128)}, u32[]{:S(2)}) copy-start(f32[512,256]{0,1:T(8,128)} %copy-done.3) | copy-start | bytes 1572868
  99.9 6.8 %copy-start.16 = (f32[512,512]{0,1:T(8,128)S(1)}, f32[512,512]{0,1:T(8,128)}, u32[]{:S(2)}) copy-start(f32[512,512]{0,1:T(8,128)} %all-reduce.6.cloned.1.call-done) | copy-start | bytes 3145732
  102.1 5.2 %copy-start.7 = (f32[256,256]{1,0:T(8,128)S(1)}, f32[256,256]{1,0:T(8,128)}, u32[]{:S(2)}) copy-start(f32[256,256]{1,0:T(8,128)} %param.29) | copy-start | bytes 786436
  105.0 4.2 %copy-start.2 = (f32[512,256]{0,1:T(8,128)S(1)}, f32[512,256]{0,1:T(8,128)}, u32[]{:S(2)}) copy-start(f32[512,256]{0,1:T(8,128)} %all_gather.10) | copy-start | bytes 1572868
  109.2 125.0 %copy-start.14 = (f32[256,256]{1,0:T(8,128)S(1)}, f32[256,256]{1,0:T(8,128)}, u32[]{:S(2)}) copy-start(f32[256,256]{1,0:T(8,128)} %param.24) | copy-start | bytes 786436
  110.9 171.2 %all-reduce.10.cloned.1.call-start = ((), (), s32[]{:S(2)}) async-start(), calls=%async_computation.4 | async-start | bytes 1572864 | tf_op jit(solution)/shard_map/psum | solution.py:25
  234.1 5.7 %copy-start.11 = (f32[256,256]{1,0:T(8,128)S(1)}, f32[256,256]{1,0:T(8,128)}, u32[]{:S(2)}) copy-start(f32[256,256]{1,0:T(8,128)} %param.18) | copy-start | bytes 786436
  234.1 5.7 %copy-start.13 = (f32[512,1024]{1,0:T(8,128)S(1)}, f32[512,1024]{1,0:T(8,128)}, u32[]{:S(2)}) copy-start(f32[512,1024]{1,0:T(8,128)} %get-tuple-element.10) | copy-start | bytes 6291460
  239.9 2.9 copy-start.1
  250.8 36.5 %copy-start.15 = (f32[256,256]{1,0:T(8,128)S(1)}, f32[256,256]{1,0:T(8,128)}, u32[]{:S(2)}) copy-start(f32[256,256]{1,0:T(8,128)} %param.25) | copy-start | bytes 786436
  250.8 37.1 %copy-start.10 = (f32[256,256]{1,0:T(8,128)S(1)}, f32[256,256]{1,0:T(8,128)}, u32[]{:S(2)}) copy-start(f32[256,256]{1,0:T(8,128)} %param.20) | copy-start | bytes 786436
  282.1 5.8 %copy-start.23 = (f32[256,256]{1,0:T(8,128)S(1)}, f32[256,256]{1,0:T(8,128)}, u32[]{:S(2)}) copy-start(f32[256,256]{1,0:T(8,128)} %get-tuple-element.16) | copy-start | bytes 786436
  282.1 6.3 %copy-start.12 = (f32[256,256]{1,0:T(8,128)S(1)}, f32[256,256]{1,0:T(8,128)}, u32[]{:S(2)}) copy-start(f32[256,256]{1,0:T(8,128)} %param.18) | copy-start | bytes 786436
  282.1 6.3 %copy-start.21 = (f32[256,256]{0,1:T(8,128)S(1)}, f32[256,256]{0,1:T(8,128)}, u32[]{:S(2)}) copy-start(f32[256,256]{0,1:T(8,128)} %get-tuple-element.11) | copy-start | bytes 786436
  285.4 4.0 %copy-start.8 = (f32[256,256]{1,0:T(8,128)S(1)}, f32[256,256]{1,0:T(8,128)}, u32[]{:S(2)}) copy-start(f32[256,256]{1,0:T(8,128)} %param.29) | copy-start | bytes 786436
  289.8 3.1 %copy-start.17 = (f32[256,256]{1,0:T(8,128)}, f32[256,256]{1,0:T(8,128)S(1)}, u32[]{:S(2)}) copy-start(f32[256,256]{1,0:T(8,128)S(1)} %fusion.39) | copy-start | bytes 786436
  (7 other events, 12.1 us)
Sparse Core Ops, SparseCore 0:
  10.1 48.7 all-gather.1
  64.8 35.0 all-reduce.5
  111.0 123.0 all-reduce.7
  248.0 34.0 all-reduce.9
